TPU v7x, 256 devices: a whole 4x4x8 slice. The times are simulated.
256 devices in a mesh: ty: 8 (over y, z_hi), tx: 16 (over x, z_lo), pa: 2 (over core).
Axes of the slice: x: 4, y: 4, z: 8 (z_hi: 2, z_lo: 4; z = z_hi * 4 + z_lo), core: 2. Of those that a mesh axis runs over, the one named last changes fastest.
Arguments:
- object_field: float32 [2, 8192, 4096], P(None, 'ty', 'tx'), may hold values from -6 to 6
- probe_field: float32 [2, 128, 128], replicated, may hold values from -6 to 6
- amplitudes: bfloat16 [8, 16, 128, 128, 128], P('ty', 'tx', 'pa'), may hold values from 0.049804688 to 1.5
- start_row: int32 [8, 16, 128], P('ty', 'tx', 'pa'), may hold values from 0 to 1023
- start_col: int32 [8, 16, 128], P('ty', 'tx', 'pa'), may hold values from 0 to 255
- counts: int32 [8, 16], replicated, may hold values from 16 to 96, as said below
Outputs:
- object_grad: float32 [2, 8192, 4096], P(None, 'ty', 'tx')
- probe_grad: float32 [2, 128, 128], replicated
Inputs may be any that keep to these rules, and one draw needn't show every extreme that they name: Tile (a, b) uses its first counts[a, b] slots; some tile uses exactly 96.
All inputs are finite; a program needn't handle non-finite values.
Results may differ from a plain program's by a relative error of at most 0.0007.
The roundings to bfloat16 on the way count: a program that leaves them out, or rounds other values in their place, can miss the bound.
Values may be sent and summed in bfloat16 or wider, within the bound.
A program may use at most 64 MiB of HBM per device.

v0:
```python
import math
import jax
import jax.numpy as jnp
from jax import lax
from jax.sharding import PartitionSpec as P

BLK = 8


def from_behind(value, axis, steps):
    count = lax.axis_size(axis)
    initial, last = (max(0, -steps), min(count, count - steps))
    return lax.ppermute(value, axis, [(source, source + steps) for source in range(initial, last)])


def dft_table(length, inverse):
    freqs = jnp.arange(length, dtype=jnp.int32)
    phase = freqs[:, None] * freqs[None, :] % length
    angle = phase.astype(jnp.float32) * (2.0 * math.pi / length)
    scale = 1.0 / math.sqrt(length)
    cosine = jnp.cos(angle) * scale
    sine = jnp.sin(angle) * scale
    if inverse:
        upper = jnp.concatenate([cosine, sine], axis=1)
        lower = jnp.concatenate([-sine, cosine], axis=1)
    else:
        upper = jnp.concatenate([cosine, -sine], axis=1)
        lower = jnp.concatenate([sine, cosine], axis=1)
    return jnp.concatenate([upper, lower], axis=0).astype(jnp.bfloat16)


def along_last(real_part, imag_part, table):
    length = real_part.shape[-1]
    stacked = jnp.concatenate([real_part, imag_part], axis=-1)
    result = jnp.einsum("bnk,kj->bnj", stacked, table, preferred_element_type=jnp.float32)
    return (result[..., :length], result[..., length:])


def patch_terms(patches, measured, probe_field, usable, forward_table, inverse_table):
    probe_re = probe_field[0]
    probe_im = probe_field[1]
    patch_re = patches[:, 0]
    patch_im = patches[:, 1]
    psi_re = (probe_re * patch_re - probe_im * patch_im).astype(jnp.bfloat16)
    psi_im = (probe_re * patch_im + probe_im * patch_re).astype(jnp.bfloat16)
    half_re, half_im = along_last(psi_re, psi_im, forward_table)
    half_re = jnp.swapaxes(half_re.astype(jnp.bfloat16), 1, 2)
    half_im = jnp.swapaxes(half_im.astype(jnp.bfloat16), 1, 2)
    wave_re, wave_im = along_last(half_re, half_im, forward_table)
    level = jnp.swapaxes(measured, 1, 2).astype(jnp.float32)
    modulus = jnp.sqrt(wave_re * wave_re + wave_im * wave_im + 1.0)
    factor = jnp.where(usable[:, None, None], 1.0 - level / modulus, 0.0)
    chi_re = (wave_re * factor).astype(jnp.bfloat16)
    chi_im = (wave_im * factor).astype(jnp.bfloat16)
    back_re, back_im = along_last(chi_re, chi_im, inverse_table)
    back_re = jnp.swapaxes(back_re.astype(jnp.bfloat16), 1, 2)
    back_im = jnp.swapaxes(back_im.astype(jnp.bfloat16), 1, 2)
    grad_re, grad_im = along_last(back_re, back_im, inverse_table)
    object_re = probe_re * grad_re + probe_im * grad_im
    object_im = probe_re * grad_im - probe_im * grad_re
    probe_part_re = jnp.sum(patch_re * grad_re + patch_im * grad_im, axis=0)
    probe_part_im = jnp.sum(patch_re * grad_im - patch_im * grad_re, axis=0)
    return (object_re, object_im, jnp.stack([probe_part_re, probe_part_im]))


def shards(object_field, probe_field, amplitudes, start_row, start_col, counts):
    width = probe_field.shape[-1]
    tile_height = object_field.shape[1]
    tile_width = object_field.shape[2]
    half = start_row.shape[-1]
    row_place = lax.axis_index("ty")
    col_place = lax.axis_index("tx")
    core_place = lax.axis_index("pa")
    count = counts[row_place, col_place]
    zero = jnp.int32(0)
    right = from_behind(object_field[:, :, :width], "tx", -1)
    wider = jnp.concatenate([object_field, right], axis=2)
    below = from_behind(wider[:, :width, :], "ty", -1)
    extended = jnp.concatenate([wider, below], axis=1)
    rows_list = start_row[0, 0]
    cols_list = start_col[0, 0]
    measured_list = amplitudes[0, 0]
    nvalid = jnp.clip(count - core_place * half, 0, half)
    forward_table = dft_table(width, False)
    inverse_table = dft_table(width, True)

    def block_step(block_index, carry):
        grad_field, probe_acc = carry
        first = block_index * BLK
        block_rows = lax.dynamic_slice_in_dim(rows_list, first, BLK)
        block_cols = lax.dynamic_slice_in_dim(cols_list, first, BLK)
        measured = lax.dynamic_slice_in_dim(measured_list, first, BLK)
        usable = first + jnp.arange(BLK, dtype=jnp.int32) < nvalid
        patches = jnp.stack(
            [
                lax.dynamic_slice(
                    extended, (zero, block_rows[member], block_cols[member]), (2, width, width)
                )
                for member in range(BLK)
            ]
        )
        object_re, object_im, probe_part = patch_terms(
            patches, measured, probe_field, usable, forward_table, inverse_table
        )
        for member in range(BLK):
            where_at = (zero, block_rows[member], block_cols[member])
            current = lax.dynamic_slice(grad_field, where_at, (2, width, width))
            added = current + jnp.stack([object_re[member], object_im[member]])
            grad_field = lax.dynamic_update_slice(grad_field, added, where_at)
        return (grad_field, probe_acc + probe_part)

    nblocks = (nvalid + BLK - 1) // BLK
    init = (jnp.zeros(extended.shape, jnp.float32), jnp.zeros((2, width, width), jnp.float32))
    grad_field, probe_acc = lax.fori_loop(0, nblocks, block_step, init)
    right_strip = grad_field[:, :, tile_width:]
    arrived = from_behind(right_strip, "tx", 1)
    grad_field = grad_field[:, :, :tile_width].at[:, :, :width].add(arrived)
    lower_strip = grad_field[:, tile_height:, :]
    arrived_below = from_behind(lower_strip, "ty", 1)
    tile_grad = grad_field[:, :tile_height, :].at[:, :width, :].add(arrived_below)
    object_grad = lax.psum(tile_grad, "pa")
    probe_total = lax.psum(probe_acc, ("ty", "tx", "pa"))
    probe_grad = probe_total / jnp.sum(counts).astype(jnp.float32)
    return (object_grad, probe_grad)


def solution(mesh):
    return jax.shard_map(
        shards,
        mesh=mesh,
        in_specs=(
            P(None, "ty", "tx"),
            P(),
            P("ty", "tx", "pa", None, None),
            P("ty", "tx", "pa"),
            P("ty", "tx", "pa"),
            P(),
        ),
        out_specs=(P(None, "ty", "tx"), P()),
        check_vma=False,
    )
```

profile of v0, /device:TPU:1, one launch (start us, length us, event | category | flops | bytes accessed | tf_op | source)
XLA Modules:
  0.0 1034.8 jit_solution(16384427669747535714)
XLA Ops:
  7.2 1.4 slice.220
  8.7 1.3 collective-permute-start
  10.0 0.1 constant_dynamic-update-slice_fusion.1
  10.1 23.9 %collective-permute-done = f32[2,1024,128]{2,1,0:T(8,128)S(1)} collective-permute-done((f32[2,1024,128]{2,1,0:T(8,128)S(1)}, f32[2,1024,128]{2,1,0:T(8,128)S(1)}, u32[]{:S(2)}, u32[]{:S(2)}) %collective-permute-start) | collective-permute-done | bytes 1048608 | tf_op jit(solution)/shard_map/ppermute | solution.py:13
  34.1 1.7 copy-done
  35.8 1.3 collective-permute-start.1
  37.1 0.6 dynamic_slice.60
  38.4 3.2 copy.10
  41.6 0.3 fusion.33
  41.9 0.3 negate_convert_fusion
  42.2 11.7 %collective-permute-done.1 = f32[2,128,384]{2,1,0:T(8,128)S(1)} collective-permute-done((f32[2,128,384]{2,1,0:T(8,128)S(1)}, f32[2,128,384]{2,1,0:T(8,128)S(1)}, u32[]{:S(2)}, u32[]{:S(2)}) %collective-permute-start.1) | collective-permute-done | bytes 393248 | tf_op jit(solution)/shard_map/ppermute | solution.py:13
  53.9 3.9 pad_maximum_fusion
  57.8 2.0 broadcast_in_dim.23
  59.8 81.8 %while.14 = (s32[]{:T(128)}, f32[2,1152,384]{2,1,0:T(8,128)}, f32[2,128,128]{2,1,0:T(8,128)S(1)}, s32[]{:T(128)}, s32[64]{0:T(128)S(1)}, /*index=5*/s32[64]{0:T(...) while((s32[]{:T(128)}, f32[2,1152,384]{2,1,0:T(8,128)}, ...), condition=%wide.region_3.4_spmd, body=%wide.region_0.3_spmd.sunk | while | flops 546603072 | bytes 25953520 | solution.py:114
  60.0 0.7 fusion.61
  62.6 0.7 fusion.60
  65.1 1.1 bitcast_dynamic-update-slice_fusion.16
  70.1 1.1 bitcast_dynamic-update-slice_fusion.17
  74.9 1.1 bitcast_dynamic-update-slice_fusion.18
  79.7 1.1 bitcast_dynamic-update-slice_fusion.19
  84.7 1.1 bitcast_dynamic-update-slice_fusion.20
  89.7 1.1 bitcast_dynamic-update-slice_fusion.21
  94.3 1.1 bitcast_dynamic-update-slice_fusion.22
  99.1 1.1 bitcast_dynamic-update-slice_fusion.23
  100.2 0.9 slice_bitcast_fusion.11
  101.1 0.2 subtract_convert_fusion.2
  101.3 0.3 convolution_convert_fusion.4
  101.6 0.1 slice_bitcast_fusion.12
  101.7 0.3 fusion.62
  102.1 0.3 multiply_convert_fusion.4
  102.3 0.3 convolution_convert_fusion.5
  102.6 0.1 slice_bitcast_fusion.13
  102.7 0.3 fusion.63
  103.1 0.3 add_reduce_fusion.2
  103.5 1.1 maximum_add_fusion.17
  104.6 3.7 dynamic_update_slice.32
  108.2 1.1 maximum_add_fusion.18
  109.3 3.7 dynamic_update_slice.33
  113.0 1.1 maximum_add_fusion.19
  114.1 3.7 dynamic_update_slice.34
  117.8 1.1 maximum_add_fusion.20
  118.9 3.7 dynamic_update_slice.35
  122.6 1.1 maximum_add_fusion.21
  123.7 3.7 dynamic_update_slice.36
  127.4 1.1 maximum_add_fusion.22
  128.5 3.7 dynamic_update_slice.37
  132.1 1.1 maximum_add_fusion.23
  133.2 3.7 dynamic_update_slice.38
  136.9 1.1 maximum_add_fusion.24
  137.9 3.7 dynamic_update_slice.39
  141.6 1.4 slice.224
  143.0 1.4 collective-permute-start.2
  144.4 1.8 slice.222
  146.2 11.2 %collective-permute-done.2 = f32[2,1152,128]{2,1,0:T(8,128)S(1)} collective-permute-done((f32[2,1152,128]{2,1,0:T(8,128)S(1)}, f32[2,1152,128]{2,1,0:T(8,128)S(1)}, u32[]{:S(2)}, u32[]{:S(2)}) %collective-permute-start.2) | collective-permute-done | bytes 1179680 | tf_op jit(solution)/shard_map/ppermute | solution.py:13
  157.4 1.4 add_dynamic-update-slice_fusion
  158.9 173.3 %collective-permute-start.3 = (f32[2,128,256]{2,1,0:T(8,128)S(1)}, f32[2,128,256]{2,1,0:T(8,128)S(1)}, u32[]{:S(2)}, u32[]{:S(2)}) collective-permute-start(f32[2,128,256]{2,1,0:T(8,128)S(1)} %slice.257), channel_id=1, source_target_pairs={{0,32},{32,64},{64,96},{96,128},{128,160},{160,192},{192,224},{1,3... | collective-permute-start | bytes 786440 | tf_op jit(solution)/shard_map/ppermute | solution.py:13
  332.2 1.5 slice.255
  333.7 1.8 collective-permute-done.3
  335.4 0.7 fusion.24
  336.2 0.7 reduce_sum.27
  337.5 654.0 %all-reduce.5.cloned.1.call-done = f32[2,128,128]{2,1,0:T(8,128)} async-done(((f32[2,128,128]{2,1,0:T(8,128)}), f32[2,128,128]{2,1,0:T(8,128)}) %all-reduce.5.cloned.1.call-update) | async-done | bytes 131088 | tf_op jit(solution)/shard_map/psum | solution.py:122
  991.4 1.6 broadcast_divide_fusion
  993.0 32.0 %all-reduce.3.cloned.1.call-done = f32[2,1024,256]{2,1,0:T(8,128)} async-done(((f32[2,1024,256]{2,1,0:T(8,128)}), f32[2,1024,256]{2,1,0:T(8,128)}) %all-reduce.3.cloned.1.call-update) | async-done | bytes 2097168 | tf_op jit(solution)/shard_map/psum | solution.py:121
  1025.0 3.0 copy.42
  (29 shorter events, 0.5 us)
Async XLA Ops:
  7.2 2.8 copy-start.2
  7.2 984.3 %all-reduce.5.cloned.1.call-start = ((), (), s32[]{:S(2)}) async-start(), calls=%async_computation.1 | async-start | bytes 262144 | tf_op jit(solution)/shard_map/psum | solution.py:122
  8.7 28.4 %copy-start.5 = (s32[8,16]{1,0:T(8,128)S(1)}, s32[8,16]{1,0:T(8,128)}, u32[]{:S(2)}) copy-start(s32[8,16]{1,0:T(8,128)} %param.17) | copy-start | bytes 1540
  8.7 25.3 %collective-permute-start = (f32[2,1024,128]{2,1,0:T(8,128)S(1)}, f32[2,1024,128]{2,1,0:T(8,128)S(1)}, u32[]{:S(2)}, u32[]{:S(2)}) collective-permute-start(f32[2,1024,128]{2,1,0:T(8,128)S(1)} %slice.220), channel_id=1, source_target_pairs={{2,0},{4,2},{6,4},{8,6},{10,8},{12,10},{14,12},{16,14},{18,16},{20... | collective-permute-start | bytes 3145736 | tf_op jit(solution)/shard_map/ppermute | solution.py:13
  34.1 1.7 copy-start
  35.8 18.1 %collective-permute-start.1 = (f32[2,128,384]{2,1,0:T(8,128)S(1)}, f32[2,128,384]{2,1,0:T(8,128)S(1)}, u32[]{:S(2)}, u32[]{:S(2)}) collective-permute-start(f32[2,128,384]{2,1,0:T(8,128)S(1)} %slice.254), channel_id=1, source_target_pairs={{32,0},{64,32},{96,64},{128,96},{160,128},{192,160},{224,192},{33,... | collective-permute-start | bytes 1179656 | tf_op jit(solution)/shard_map/ppermute | solution.py:13
  57.8 2.1 copy-start.6
  57.8 2.1 copy-start.7
  59.9 43.6 %copy-start.3 = (bf16[256,256]{1,0:T(8,128)(2,1)}, bf16[256,256]{1,0:T(8,128)(2,1)S(1)}, u32[]{:S(2)}) copy-start(bf16[256,256]{1,0:T(8,128)(2,1)S(1)} %get-tuple-element.384) | copy-start | bytes 393220 | tf_op jit(solution)/shard_map/while
  114.1 27.5 %copy-start.4 = (bf16[256,256]{1,0:T(8,128)(2,1)S(1)}, bf16[256,256]{1,0:T(8,128)(2,1)}, u32[]{:S(2)}) copy-start(bf16[256,256]{1,0:T(8,128)(2,1)} %copy-done.3) | copy-start | bytes 393220 | tf_op jit(solution)/shard_map/while
  141.6 4.6 copy-start.1
  143.0 14.4 %collective-permute-start.2 = (f32[2,1152,128]{2,1,0:T(8,128)S(1)}, f32[2,1152,128]{2,1,0:T(8,128)S(1)}, u32[]{:S(2)}, u32[]{:S(2)}) collective-permute-start(f32[2,1152,128]{2,1,0:T(8,128)S(1)} %slice.224), channel_id=1, source_target_pairs={{0,2},{2,4},{4,6},{6,8},{8,10},{10,12},{12,14},{14,16},{16,18},{18... | collective-permute-start | bytes 3538952 | tf_op jit(solution)/shard_map/ppermute | solution.py:13
  158.9 176.6 %collective-permute-start.3 = (f32[2,128,256]{2,1,0:T(8,128)S(1)}, f32[2,128,256]{2,1,0:T(8,128)S(1)}, u32[]{:S(2)}, u32[]{:S(2)}) collective-permute-start(f32[2,128,256]{2,1,0:T(8,128)S(1)} %slice.257), channel_id=1, source_target_pairs={{0,32},{32,64},{64,96},{96,128},{128,160},{160,192},{192,224},{1,3... | collective-permute-start | bytes 786440 | tf_op jit(solution)/shard_map/ppermute | solution.py:13
  332.2 692.8 %all-reduce.3.cloned.1.call-start = ((), (), s32[]{:S(2)}) async-start(), calls=%async_computation | async-start | bytes 4194304 | tf_op jit(solution)/shard_map/psum | solution.py:121
Sparse Core Ops, SparseCore 0:
  332.3 659.1 all-reduce.4
  994.6 30.3 all-reduce.2
where the time goes:
time: 1050 us; the launch traced here: 1030 us
  waiting for transfers between devices  734 us (70%)
  starting transfers between devices  177 us (17%)
  local copies, waits for them, and re-layouts  57.8 us (6%)
  loops' own time  30.4 us (3%)
  other arithmetic  18 us (2%)
  between operations  15.5 us (1%)
    psum x1, waiting for transfers between devices, shards(): probe_total = lax.psum(probe_acc, ('ty', 'tx', 'pa'))  654 us
    ppermute x4, starting transfers between devices, from_behind(): lax.ppermute(value, axis, [(source, source + steps) for source in range(i...  177 us
    ppermute x4, waiting for transfers between devices, from_behind(): lax.ppermute(value, axis, [(source, source + steps) for source in range(i...  48.5 us
    psum x1, waiting for transfers between devices, shards(): object_grad = lax.psum(tile_grad, 'pa')  32 us
    another operation x1, loops' own time, shards(): grad_field, probe_acc = lax.fori_loop(0, nblocks, block_step, init)  30.4 us
    dynamic_update_slice x8, local copies, waits for them, and re-layouts, block_step(): grad_field = lax.dynamic_update_slice(grad_field, added, where_at)  29.6 us
  transfers between devices with their start and end apart: 6, of which 6 were waited for; matrix products, arithmetic and copies ran while one was open for 1% of the time, Pallas kernels for 0%

commit v1 on v0

--- a/solution.py
+++ b/solution.py
@@ -118,7 +118,8 @@
     lower_strip = grad_field[:, tile_height:, :]
     arrived_below = from_behind(lower_strip, "ty", 1)
     tile_grad = grad_field[:, :tile_height, :].at[:, :width, :].add(arrived_below)
-    object_grad = lax.psum(tile_grad, "pa")
+    base_arr = lax.all_gather(tile_grad, "pa")
+    object_grad = jnp.sum(base_arr, axis=0)
     probe_total = lax.psum(probe_acc, ("ty", "tx", "pa"))
     probe_grad = probe_total / jnp.sum(counts).astype(jnp.float32)
     return (object_grad, probe_grad)

time: 1050 us -> 1000 us (0.952)
  waiting for transfers between devices: 734 us -> 682 us
    psum x1 -> x0, waiting for transfers between devices: 32 us -> none  [shards(): object_grad = lax.psum(tile_grad, 'pa')]
    psum x1, waiting for transfers between devices: 654 us -> 634 us  [shards(): probe_total = lax.psum(probe_acc, ('ty', 'tx', 'pa'))]
  transfers between devices with their start and end apart: 6 -> 6, of which waited for: 6 -> 5; matrix products, arithmetic and copies ran while one was open for 1% -> 1% of each run, Pallas kernels for 0% -> 0%
where the time goes in v1:
time: 1000 us; the launch traced here: 987 us
  waiting for transfers between devices  682 us (68%)
  starting transfers between devices  178 us (18%)
  local copies, waits for them, and re-layouts  55.8 us (6%)
  loops' own time  30.4 us (3%)
  other arithmetic  22.4 us (2%)
  between operations  17 us (2%)
    psum x1, waiting for transfers between devices, shards(): probe_total = lax.psum(probe_acc, ('ty', 'tx', 'pa'))  634 us
    ppermute x4, starting transfers between devices, from_behind(): lax.ppermute(value, axis, [(source, source + steps) for source in range(i...  178 us
    ppermute x4, waiting for transfers between devices, from_behind(): lax.ppermute(value, axis, [(source, source + steps) for source in range(i...  47.9 us
    another operation x1, loops' own time, shards(): grad_field, probe_acc = lax.fori_loop(0, nblocks, block_step, init)  30.4 us
    dynamic_update_slice x8, local copies, waits for them, and re-layouts, block_step(): grad_field = lax.dynamic_update_slice(grad_field, added, where_at)  29.6 us
  transfers between devices with their start and end apart: 6, of which 5 were waited for; matrix products, arithmetic and copies ran while one was open for 1% of the time, Pallas kernels for 0%

profile of v1, /device:TPU:1, one launch (start us, length us, event | category | flops | bytes accessed | tf_op | source)
XLA Modules:
  0.0 987.0 jit_solution(9865679673370901483)
XLA Ops:
  8.1 1.4 slice.220
  9.5 1.3 collective-permute-start
  10.8 0.1 constant_dynamic-update-slice_fusion.1
  11.0 23.9 %collective-permute-done = f32[2,1024,128]{2,1,0:T(8,128)S(1)} collective-permute-done((f32[2,1024,128]{2,1,0:T(8,128)S(1)}, f32[2,1024,128]{2,1,0:T(8,128)S(1)}, u32[]{:S(2)}, u32[]{:S(2)}) %collective-permute-start) | collective-permute-done | bytes 1048608 | tf_op jit(solution)/shard_map/ppermute | solution.py:13
  34.9 1.7 copy-done
  36.6 1.3 collective-permute-start.1
  37.9 0.6 dynamic_slice.60
  39.2 3.2 copy.13
  42.5 0.3 fusion.34
  42.7 0.3 negate_convert_fusion
  43.0 11.7 %collective-permute-done.1 = f32[2,128,384]{2,1,0:T(8,128)S(1)} collective-permute-done((f32[2,128,384]{2,1,0:T(8,128)S(1)}, f32[2,128,384]{2,1,0:T(8,128)S(1)}, u32[]{:S(2)}, u32[]{:S(2)}) %collective-permute-start.1) | collective-permute-done | bytes 393248 | tf_op jit(solution)/shard_map/ppermute | solution.py:13
  54.7 3.9 pad_maximum_fusion
  58.6 2.0 broadcast_in_dim.23
  60.7 81.8 %while.14 = (s32[]{:T(128)}, f32[2,1152,384]{2,1,0:T(8,128)}, f32[2,128,128]{2,1,0:T(8,128)S(1)}, s32[]{:T(128)}, s32[64]{0:T(128)S(1)}, /*index=5*/s32[64]{0:T(...) while((s32[]{:T(128)}, f32[2,1152,384]{2,1,0:T(8,128)}, ...), condition=%wide.region_3.4_spmd, body=%wide.region_0.3_spmd.sunk | while | flops 546603072 | bytes 25953520 | solution.py:114
  60.8 0.7 fusion.62
  63.3 0.1 dynamic_slice.115
  63.4 0.7 fusion.61
  66.0 1.1 bitcast_dynamic-update-slice_fusion.16
  70.9 1.1 bitcast_dynamic-update-slice_fusion.17
  75.7 1.1 bitcast_dynamic-update-slice_fusion.18
  80.5 1.1 bitcast_dynamic-update-slice_fusion.19
  85.5 1.1 bitcast_dynamic-update-slice_fusion.20
  90.5 1.1 bitcast_dynamic-update-slice_fusion.21
  95.1 1.1 bitcast_dynamic-update-slice_fusion.22
  100.0 1.1 bitcast_dynamic-update-slice_fusion.23
  101.0 0.9 slice_bitcast_fusion.12
  101.9 0.2 subtract_convert_fusion.2
  102.1 0.3 convolution_convert_fusion.4
  102.4 0.1 slice_bitcast_fusion.13
  102.5 0.3 fusion.63
  102.9 0.3 multiply_convert_fusion.4
  103.2 0.3 convolution_convert_fusion.5
  103.5 0.1 slice_bitcast_fusion.14
  103.6 0.3 fusion.64
  103.9 0.3 add_reduce_fusion.2
  104.3 1.1 maximum_add_fusion.17
  105.4 3.7 dynamic_update_slice.32
  109.1 1.1 maximum_add_fusion.18
  110.2 3.7 dynamic_update_slice.33
  113.9 1.1 maximum_add_fusion.19
  114.9 3.7 dynamic_update_slice.34
  118.7 1.1 maximum_add_fusion.20
  119.8 3.7 dynamic_update_slice.35
  123.5 1.1 maximum_add_fusion.21
  124.6 3.7 dynamic_update_slice.36
  128.3 1.1 maximum_add_fusion.22
  129.3 3.7 dynamic_update_slice.37
  133.0 1.1 maximum_add_fusion.23
  134.1 3.7 dynamic_update_slice.38
  137.7 1.1 maximum_add_fusion.24
  138.8 3.7 dynamic_update_slice.39
  142.5 2.4 slice.224
  144.9 2.3 collective-permute-start.2
  147.2 1.8 slice.222
  149.1 10.5 %collective-permute-done.2 = f32[2,1152,128]{2,1,0:T(8,128)} collective-permute-done((f32[2,1152,128]{2,1,0:T(8,128)}, f32[2,1152,128]{2,1,0:T(8,128)}, u32[]{:S(2)}, u32[]{:S(2)}) %collective-permute-start.2) | collective-permute-done | bytes 1179680 | tf_op jit(solution)/shard_map/ppermute | solution.py:13
  159.6 1.8 add_dynamic-update-slice_fusion
  161.4 173.3 %collective-permute-start.3 = (f32[2,128,256]{2,1,0:T(8,128)S(1)}, f32[2,128,256]{2,1,0:T(8,128)S(1)}, u32[]{:S(2)}, u32[]{:S(2)}) collective-permute-start(f32[2,128,256]{2,1,0:T(8,128)S(1)} %slice.257), channel_id=1, source_target_pairs={{0,32},{32,64},{64,96},{96,128},{128,160},{160,192},{192,224},{1,3... | collective-permute-start | bytes 786440 | tf_op jit(solution)/shard_map/ppermute | solution.py:13
  334.7 1.5 slice_bitcast_fusion.8
  336.1 1.8 collective-permute-done.3
  338.0 0.7 fusion.25
  338.7 0.7 reduce_sum.37
  340.0 633.9 %all-reduce.2.cloned.1.call-done = f32[2,128,128]{2,1,0:T(8,128)} async-done(((f32[2,128,128]{2,1,0:T(8,128)}), f32[2,128,128]{2,1,0:T(8,128)}) %all-reduce.2.cloned.1.call-update) | async-done | bytes 131088 | tf_op jit(solution)/shard_map/psum | solution.py:123
  973.9 1.6 broadcast_divide_fusion
  975.5 4.0 reduce_sum.36
  (29 shorter events, 0.5 us)
Async XLA Ops:
  8.0 2.8 copy-start.2
  8.0 965.9 %all-reduce.2.cloned.1.call-start = ((), (), s32[]{:S(2)}) async-start(), calls=%async_computation.1 | async-start | bytes 262144 | tf_op jit(solution)/shard_map/psum | solution.py:123
  9.5 28.4 %copy-start.5 = (s32[8,16]{1,0:T(8,128)S(1)}, s32[8,16]{1,0:T(8,128)}, u32[]{:S(2)}) copy-start(s32[8,16]{1,0:T(8,128)} %param.17) | copy-start | bytes 1540
  9.5 25.3 %collective-permute-start = (f32[2,1024,128]{2,1,0:T(8,128)S(1)}, f32[2,1024,128]{2,1,0:T(8,128)S(1)}, u32[]{:S(2)}, u32[]{:S(2)}) collective-permute-start(f32[2,1024,128]{2,1,0:T(8,128)S(1)} %slice.220), channel_id=1, source_target_pairs={{2,0},{4,2},{6,4},{8,6},{10,8},{12,10},{14,12},{16,14},{18,16},{20... | collective-permute-start | bytes 3145736 | tf_op jit(solution)/shard_map/ppermute | solution.py:13
  34.9 1.7 copy-start
  36.6 18.1 %collective-permute-start.1 = (f32[2,128,384]{2,1,0:T(8,128)S(1)}, f32[2,128,384]{2,1,0:T(8,128)S(1)}, u32[]{:S(2)}, u32[]{:S(2)}) collective-permute-start(f32[2,128,384]{2,1,0:T(8,128)S(1)} %slice.254), channel_id=1, source_target_pairs={{32,0},{64,32},{96,64},{128,96},{160,128},{192,160},{224,192},{33,... | collective-permute-start | bytes 1179656 | tf_op jit(solution)/shard_map/ppermute | solution.py:13
  58.6 2.1 copy-start.6
  58.6 2.1 copy-start.7
  60.7 43.6 %copy-start.3 = (bf16[256,256]{1,0:T(8,128)(2,1)}, bf16[256,256]{1,0:T(8,128)(2,1)S(1)}, u32[]{:S(2)}) copy-start(bf16[256,256]{1,0:T(8,128)(2,1)S(1)} %get-tuple-element.384) | copy-start | bytes 393220 | tf_op jit(solution)/shard_map/while
  114.9 27.5 %copy-start.4 = (bf16[256,256]{1,0:T(8,128)(2,1)S(1)}, bf16[256,256]{1,0:T(8,128)(2,1)}, u32[]{:S(2)}) copy-start(bf16[256,256]{1,0:T(8,128)(2,1)} %copy-done.3) | copy-start | bytes 393220 | tf_op jit(solution)/shard_map/while
  142.4 6.6 copy-start.1
  144.9 14.7 %collective-permute-start.2 = (f32[2,1152,128]{2,1,0:T(8,128)}, f32[2,1152,128]{2,1,0:T(8,128)}, u32[]{:S(2)}, u32[]{:S(2)}) collective-permute-start(f32[2,1152,128]{2,1,0:T(8,128)} %slice.224), channel_id=1, source_target_pairs={{0,2},{2,4},{4,6},{6,8},{8,10},{10,12},{12,14},{14,16},{16,18},{18... | collective-permute-start | bytes 3538952 | tf_op jit(solution)/shard_map/ppermute | solution.py:13
  149.0 826.4 %all-gather.2.cloned.1.call-start = ((), (), s32[]{:S(2)}) async-start(), calls=%async_computation | async-start | bytes 6291456 | tf_op jit(solution)/shard_map/all_gather | solution.py:121
  161.4 176.6 %collective-permute-start.3 = (f32[2,128,256]{2,1,0:T(8,128)S(1)}, f32[2,128,256]{2,1,0:T(8,128)S(1)}, u32[]{:S(2)}, u32[]{:S(2)}) collective-permute-start(f32[2,128,256]{2,1,0:T(8,128)S(1)} %slice.257), channel_id=1, source_target_pairs={{0,32},{32,64},{64,96},{96,128},{128,160},{160,192},{192,224},{1,3... | collective-permute-start | bytes 786440 | tf_op jit(solution)/shard_map/ppermute | solution.py:13
Sparse Core Ops, SparseCore 0:
  149.2 824.6 all-reduce.1
Sparse Core Ops, SparseCore 1:
  338.8 444.2 all-gather.1
